TPU v7x, 128 devices: a whole 4x4x4 slice. The times are simulated.
128 devices in a mesh: req: 16 (over y, x), hid: 8 (over z, core).
Axes of the slice: x: 4, y: 4, z: 4, core: 2. Of those that a mesh axis runs over, the one named last changes fastest.
Arguments:
- tokens: bfloat16 [32, 16, 2, 4096], P('req', 'hid'), may hold values from -6 to 6
- input_gain: float32 [4096], replicated, may hold values from 0.1 to 1.9
- qkv_weight: bfloat16 [4096, 3, 4096], P(None, None, 'hid'), may hold values from -0.09375 to 0.09375
- out_weight: bfloat16 [4096, 4096], P('hid'), may hold values from -0.375 to 0.375
- in_weight: bfloat16 [4096, 16384], P(None, ('req', 'hid')), may hold values from -0.09375 to 0.09375
- down_weight: bfloat16 [16384, 4096], P(('req', 'hid')), may hold values from -0.046875 to 0.046875
- final_gain: float32 [4096], replicated, may hold values from 0.1 to 1.9
- score_weight: bfloat16 [4096], replicated, may hold values from -0.09375 to 0.09375
- prompt_keys: bfloat16 [32, 2048, 4096], P('req', None, 'hid'), may hold values from -260 to 260
- prompt_values: bfloat16 [32, 2048, 4096], P('req', None, 'hid'), may hold values from -6 to 6
- tail_keys: bfloat16 [32, 16, 64, 4096], P('req', None, None, 'hid'), may hold values from -12 to 12
- tail_values: bfloat16 [32, 16, 64, 4096], P('req', None, None, 'hid'), may hold values from -6 to 6
- prompt_lengths: int32 [32], P('req'), may hold values from 1 to 2048
- tail_lengths: int32 [32, 16], P('req'), may hold values from 0 to 64
Outputs:
- next_hidden: bfloat16 [32, 16, 2, 4096], P('req', 'hid')
- sample_scores: float32 [32, 16, 2], P('req', 'hid')
Inputs may be any that keep to these rules, and one draw needn't show every extreme that they name: `prompt_lengths`: a request's prompt occupies positions 0 to its length - 1. `tail_lengths`: a sample's tail occupies positions 0 to its length - 1.
All inputs are finite; a program needn't handle non-finite values.
Results may differ from a plain program's by a relative error of at most 0.017.
Values may be sent and summed in bfloat16 or wider, within the bound.
No kernel may reach another device: no remote copies, remote signals or barrier semaphores. Data moves between devices by JAX's collectives and lax.ppermute only.
A program may use at most 128 MiB of HBM per device.

v0:
```python
import jax
import jax.numpy as jnp
from jax import lax
from jax.sharding import PartitionSpec as P

HEAD_DIM = 256
ROT = 64
very_low = -1e30


def layer_norm(values, gain):
    centre = jnp.mean(values, axis=-1, keepdims=True)
    centred = values - centre
    spread = jnp.mean(centred * centred, axis=-1, keepdims=True)
    return centred * lax.rsqrt(spread + 1e-05) * gain


def rotate(vectors, positions):
    half_rot = ROT // 2
    frequency = 10000.0 ** (-(jnp.arange(half_rot, dtype=jnp.float32) * (2.0 / ROT)))
    angles = positions.astype(jnp.float32)[..., None] * frequency
    cosine = jnp.cos(angles)[..., None, :]
    sine_part = jnp.sin(angles)[..., None, :]
    paired = vectors[..., :ROT].reshape(vectors.shape[:-1] + (half_rot, 2))
    even_part = paired[..., 0]
    odd_part = paired[..., 1]
    turned = jnp.stack(
        [even_part * cosine - odd_part * sine_part, odd_part * cosine + even_part * sine_part],
        axis=-1,
    )
    return jnp.concatenate(
        [turned.reshape(vectors.shape[:-1] + (ROT,)), vectors[..., ROT:]], axis=-1
    )


def shards(
    tokens,
    input_gain,
    qkv_weight,
    out_weight,
    in_weight,
    down_weight,
    final_gain,
    score_weight,
    prompt_keys,
    prompt_values,
    tail_keys,
    tail_values,
    prompt_lengths,
    tail_lengths,
):
    req_dev, samp_dev, fresh, width = tokens.shape
    own_rows = req_dev * samp_dev * fresh
    residual = tokens.astype(jnp.float32).reshape(own_rows, width)
    normed = layer_norm(residual, input_gain).astype(jnp.bfloat16)
    gathered = lax.all_gather(normed, ("req", "hid"), axis=0, tiled=True)
    hidden_units = jax.nn.gelu(
        jnp.dot(gathered, in_weight, preferred_element_type=jnp.float32), approximate=True
    ).astype(jnp.bfloat16)
    slab_rows, triple, slab_cols = qkv_weight.shape
    flat_qkv = qkv_weight.reshape(slab_rows, triple * slab_cols)
    hid_count = lax.axis_size("hid")
    group_rows = own_rows * hid_count
    group_normed = lax.dynamic_slice_in_dim(
        gathered, lax.axis_index("req") * group_rows, group_rows, 0
    )
    mixed_qkv = jnp.dot(group_normed, flat_qkv, preferred_element_type=jnp.float32).astype(
        jnp.bfloat16
    )
    heads_here = slab_cols // HEAD_DIM
    samples = hid_count * samp_dev
    grouped = mixed_qkv.reshape(hid_count, req_dev, samp_dev, fresh, triple, heads_here, HEAD_DIM)
    grouped = jnp.transpose(grouped, (1, 0, 2, 3, 4, 5, 6)).reshape(
        req_dev, samples, fresh, triple, heads_here, HEAD_DIM
    )
    positions = (
        prompt_lengths[:, None, None]
        + tail_lengths[:, :, None]
        + jnp.arange(fresh, dtype=jnp.int32)[None, None, :]
    )
    queries = rotate(grouped[:, :, :, 0].astype(jnp.float32), positions).astype(jnp.bfloat16)
    new_keys = rotate(grouped[:, :, :, 1].astype(jnp.float32), positions).astype(jnp.bfloat16)
    new_values = grouped[:, :, :, 2]
    prompt_len = prompt_keys.shape[1]
    cached_keys = prompt_keys.reshape(req_dev, prompt_len, heads_here, HEAD_DIM)
    cached_values = prompt_values.reshape(req_dev, prompt_len, heads_here, HEAD_DIM)
    prompt_queries = queries.reshape(req_dev, samples * fresh, heads_here, HEAD_DIM)
    score_scale = HEAD_DIM ** (-0.5)
    prompt_scores = (
        jnp.einsum(
            "rqhd,rkhd->rqhk", prompt_queries, cached_keys, preferred_element_type=jnp.float32
        )
        * score_scale
    )
    keeping = (jnp.arange(prompt_len, dtype=jnp.int32)[None, :] < prompt_lengths[:, None])[
        :, None, None, :
    ]
    prompt_scores = jnp.where(keeping, prompt_scores, very_low)
    peaks = jnp.max(prompt_scores, axis=-1)
    prompt_weights = jnp.where(keeping, jnp.exp(prompt_scores - peaks[..., None]), 0.0)
    totals = jnp.sum(prompt_weights, axis=-1)
    accrued = jnp.einsum(
        "rqhk,rkhd->rqhd",
        prompt_weights.astype(jnp.bfloat16),
        cached_values,
        preferred_element_type=jnp.float32,
    )
    peaks = peaks.reshape(req_dev, samples, fresh, heads_here)
    totals = totals.reshape(req_dev, samples, fresh, heads_here)
    accrued = accrued.reshape(req_dev, samples, fresh, heads_here, HEAD_DIM)
    tail_len = tail_keys.shape[2]
    later_keys = tail_keys.reshape(req_dev, samples, tail_len, heads_here, HEAD_DIM)
    later_values = tail_values.reshape(req_dev, samples, tail_len, heads_here, HEAD_DIM)
    tail_scores = (
        jnp.einsum("rsthd,rskhd->rsthk", queries, later_keys, preferred_element_type=jnp.float32)
        * score_scale
    )
    tail_keep = (jnp.arange(tail_len, dtype=jnp.int32)[None, None, :] < tail_lengths[:, :, None])[
        :, :, None, None, :
    ]
    self_scores = (
        jnp.einsum("rsthd,rsuhd->rsthu", queries, new_keys, preferred_element_type=jnp.float32)
        * score_scale
    )
    position_order = jnp.arange(fresh, dtype=jnp.int32)
    self_keep = (position_order[None, :] <= position_order[:, None])[None, None, :, None, :]
    highest = jnp.maximum(peaks, jnp.max(jnp.where(tail_keep, tail_scores, very_low), axis=-1))
    highest = jnp.maximum(highest, jnp.max(jnp.where(self_keep, self_scores, very_low), axis=-1))
    scaling = jnp.exp(peaks - highest)
    tail_weights = jnp.where(tail_keep, jnp.exp(tail_scores - highest[..., None]), 0.0)
    self_weights = jnp.where(self_keep, jnp.exp(self_scores - highest[..., None]), 0.0)
    totals = totals * scaling + jnp.sum(tail_weights, axis=-1) + jnp.sum(self_weights, axis=-1)
    accrued = accrued * scaling[..., None]
    accrued = accrued + jnp.einsum(
        "rsthk,rskhd->rsthd",
        tail_weights.astype(jnp.bfloat16),
        later_values,
        preferred_element_type=jnp.float32,
    )
    accrued = accrued + jnp.einsum(
        "rsthu,rsuhd->rsthd",
        self_weights.astype(jnp.bfloat16),
        new_values,
        preferred_element_type=jnp.float32,
    )
    attended = (accrued / totals[..., None]).astype(jnp.bfloat16)
    attended = attended.reshape(req_dev, hid_count, samp_dev, fresh, heads_here * HEAD_DIM)
    attended_rows = jnp.transpose(attended, (1, 0, 2, 3, 4)).reshape(
        group_rows, heads_here * HEAD_DIM
    )
    mlp_part = lax.psum_scatter(
        jnp.dot(hidden_units, down_weight, preferred_element_type=jnp.float32),
        ("req", "hid"),
        scatter_dimension=0,
        tiled=True,
    )
    projection_part = lax.psum_scatter(
        jnp.dot(attended_rows, out_weight, preferred_element_type=jnp.float32).astype(jnp.bfloat16),
        "hid",
        scatter_dimension=0,
        tiled=True,
    ).astype(jnp.float32)
    branch_sum = mlp_part + projection_part
    final_state = residual + branch_sum
    next_hidden = final_state.astype(jnp.bfloat16).reshape(req_dev, samp_dev, fresh, width)
    sample_scores = jnp.sum(
        layer_norm(final_state, final_gain) * score_weight.astype(jnp.float32), axis=-1
    )
    return (next_hidden, sample_scores.reshape(req_dev, samp_dev, fresh))


def solution(mesh):
    placed = (
        P("req", "hid", None, None),
        P(),
        P(None, None, "hid"),
        P("hid", None),
        P(None, ("req", "hid")),
        P(("req", "hid"), None),
        P(),
        P(),
        P("req", None, "hid"),
        P("req", None, "hid"),
        P("req", None, None, "hid"),
        P("req", None, None, "hid"),
        P("req"),
        P("req", None),
    )
    return jax.shard_map(
        shards,
        mesh=mesh,
        in_specs=placed,
        out_specs=(P("req", "hid", None, None), P("req", "hid", None)),
        check_vma=False,
    )
```

profile of v0, /device:TPU:0, one launch (start us, length us, event | category | flops | bytes accessed | tf_op | source)
XLA Modules:
  0.0 822.6 jit_solution(10335013178201926168)
XLA Ops:
  7.2 0.9 reshape.217
  8.2 1.0 convert_reduce_fusion
  9.2 1.1 multiply_reduce_fusion.2
  10.2 0.1 div.23
  10.3 0.1 rsqrt.20
  10.4 1.4 multiply_convert_fusion
  11.9 0.0 reduce-scatter.5.cloned.1.call-start
  12.0 16.9 %copy.120 = bf16[4096,3,512]{0,2,1:T(8,128)(2,1)} copy(bf16[4096,3,512]{2,0,1:T(8,128)(2,1)} %param.16) | data formatting | bytes 25165824 | tf_op args[2]
  28.9 0.1 broadcast_add_fusion
  29.0 0.1 iota_compare_fusion
  29.1 0.3 multiply_cosine_fusion
  29.4 0.1 iota_compare_fusion.1
  29.5 55.2 %all-gather.2.cloned.1.call-done = bf16[1024,4096]{1,0:T(8,128)(2,1)} async-done(((bf16[8,4096]{1,0:T(8,128)(2,1)}), bf16[1024,4096]{1,0:T(8,128)(2,1)}) %all-gather.2.cloned.1.call-update) | async-done | bytes 8388624 | tf_op jit(solution)/shard_map/all_gather | solution.py:56
  84.7 8.7 %convolution_convert_fusion.1 = bf16[64,1536]{1,0:T(8,128)(2,1)S(1)} fusion(bf16[4096,1536]{0,1:T(8,128)(2,1)} %bitcast.109, bf16[1024,4096]{1,0:T(8,128)(2,1)} %all-gather.2.cloned.1.call-done, s32[]{:T(128)S(6)} %select_n.27), kind=kOutput, calls=%fused_computation.10 | convolution fusion | flops 805404672 | bytes 13303812 | tf_op jit(solution)/shard_map/dot_general | solution.py:67
  93.3 0.1 reshape.219
  93.4 0.2 copy.209
  93.6 0.1 reshape.220
  93.7 0.1 slice.72
  93.8 0.1 slice.55
  93.9 0.1 copy.122
  94.1 0.3 multiply_subtract_fusion
  94.4 0.4 maximum_convert_fusion
  94.8 2.0 copy.123
  96.8 0.1 copy.128
  96.9 0.1 copy.133
  97.0 0.3 subtract_convert_fusion
  97.4 0.4 pad_maximum_fusion
  97.7 0.1 copy.134
  97.9 0.1 copy.124
  97.9 0.1 pad_maximum_fusion.1
  98.0 0.2 fusion.65
  98.2 0.1 copy.137
  98.4 2.4 select_reduce_fusion
  100.7 0.1 copy.132
  100.8 1.9 concatenate.16
  102.8 3.6 fusion.85
  106.4 0.1 reshape.225
  106.5 0.1 copy.140
  106.6 0.1 fusion.70
  106.7 0.1 copy.143
  106.8 0.1 fusion.83
  106.9 0.3 fusion.73
  107.2 0.1 copy.148
  107.3 0.3 fusion.39
  107.6 0.1 reshape.232
  107.7 0.1 copy.147
  107.8 0.1 copy.141
  107.9 3.0 fusion.21
  111.0 0.1 reshape.224
  111.1 0.1 copy.151
  111.2 0.1 copy.146
  111.3 2.0 fusion.29
  113.4 0.2 fusion.32
  113.7 4.1 convolution_convert_fusion
  117.8 0.0 reduce-scatter.3.cloned.1.call-start
  117.8 14.4 %fusion.54 = f32[1024,4096]{1,0:T(8,128)} fusion(bf16[128,4096]{1,0:T(8,128)(2,1)S(1)} %copy-done, bf16[1024,4096]{1,0:T(8,128)(2,1)} %all-gather.2.cloned.1.call-done, bf16[4096,128]{1,0:T(8,128)(2,1)S(1)} %copy-done.1), kind=kOutput, calls=%fused_computation.42 | convolution fusion | flops 2148663296 | bytes 27262976 | tf_op jit(solution)/shard_map/dot_general | solution.py:152
  132.2 0.7 copy-done.3
  132.9 13.7 %reduce-scatter.5.cloned.1.call-done = bf16[8,4096]{1,0:T(8,128)(2,1)} async-done(((bf16[64,4096]{1,0:T(8,128)(2,1)}), bf16[8,4096]{1,0:T(8,128)(2,1)}) %reduce-scatter.5.cloned.1.call-update) | async-done | bytes 65552 | tf_op jit(solution)/shard_map/reduce_scatter | solution.py:157
  146.6 666.6 %reduce-scatter.3.cloned.1.call-done = f32[8,4096]{1,0:T(8,128)} async-done(((f32[1024,4096]{1,0:T(8,128)}), f32[8,4096]{1,0:T(8,128)}) %reduce-scatter.3.cloned.1.call-update) | async-done | bytes 131088 | tf_op jit(solution)/shard_map/reduce_scatter | solution.py:151
  813.2 1.1 fusion.84
  814.2 0.2 multiply_reduce_fusion.1
  814.5 0.2 multiply_reduce_fusion
  814.7 0.7 reshape.235
  815.4 0.7 reshape.236
  (31 shorter events, 0.3 us)
Async XLA Ops:
  7.2 110.6 %copy-start = (bf16[128,4096]{1,0:T(8,128)(2,1)S(1)}, bf16[128,4096]{1,0:T(8,128)(2,1)}, u32[]{:S(2)}) copy-start(bf16[128,4096]{1,0:T(8,128)(2,1)} %param.19) | copy-start | bytes 3145732
  7.2 77.5 %all-gather.2.cloned.1.call-start = ((), (), s32[]{:S(2)}) async-start(), calls=%async_computation.2 | async-start | bytes 8454144 | tf_op jit(solution)/shard_map/all_gather | solution.py:56
  11.9 134.7 %reduce-scatter.5.cloned.1.call-start = ((), (), s32[]{:S(2)}) async-start(), calls=%async_computation.4 | async-start | bytes 589824 | tf_op jit(solution)/shard_map/reduce_scatter | solution.py:157
  11.9 17.0 %copy-start.4 = (s32[2,16]{1,0:T(2,128)S(1)}, s32[2,16]{1,0:T(2,128)}, u32[]{:S(2)}) copy-start(s32[2,16]{1,0:T(2,128)} %param.27) | copy-start | bytes 388
  11.9 17.0 %copy-start.5 = (s32[2]{0:T(128)S(1)}, s32[2]{0:T(128)}, u32[]{:S(2)}) copy-start(s32[2]{0:T(128)} %param.26) | copy-start | bytes 28
  113.3 4.5 copy-start.1
  117.8 695.4 %reduce-scatter.3.cloned.1.call-start = ((), (), s32[]{:S(2)}) async-start(), calls=%async_computation.3 | async-start | bytes 16908288 | tf_op jit(solution)/shard_map/reduce_scatter | solution.py:151
  132.2 0.7 copy-start.3
  132.2 682.2 %copy-start.2 = (f32[4096]{0:T(1024)S(1)}, f32[4096]{0:T(1024)}, u32[]{:S(2)}) copy-start(f32[4096]{0:T(1024)} %param.20) | copy-start | bytes 49156
Sparse Core Ops, SparseCore 0:
  12.0 72.6 all-gather.1
  117.9 28.6 reduce-scatter.4
  149.1 664.0 reduce-scatter.2
where the time goes:
time: 823 us
  waiting for transfers between devices  735 us (89%)
  matrix products  38.6 us (5%)
  local copies, waits for them, and re-layouts  26.3 us (3%)
  between operations  14.1 us (2%)
    reduce_scatter x1, waiting for transfers between devices, shards(): lax.psum_scatter(jnp.dot(hidden_units, down_weight, preferred_element_typ...  667 us
    all_gather x1, waiting for transfers between devices, shards(): gathered = lax.all_gather(normed, ('req', 'hid'), axis=0, tiled=True)  55.2 us
    unnamed x13, local copies, waits for them, and re-layouts  17.6 us
  transfers between devices with their start and end apart: 3, of which 3 were waited for; matrix products, arithmetic and copies ran while one was open for 4% of the time, Pallas kernels for 0%

commit v1 on v0

--- a/solution.py
+++ b/solution.py
@@ -53,7 +53,10 @@
     own_rows = req_dev * samp_dev * fresh
     residual = tokens.astype(jnp.float32).reshape(own_rows, width)
     normed = layer_norm(residual, input_gain).astype(jnp.bfloat16)
-    gathered = lax.all_gather(normed, ("req", "hid"), axis=0, tiled=True)
+    gathered = jnp.concatenate(
+        lax.all_to_all(jnp.stack([normed] * lax.axis_size(("req", "hid"))), ("req", "hid"), 0, 0),
+        axis=0,
+    )
     hidden_units = jax.nn.gelu(
         jnp.dot(gathered, in_weight, preferred_element_type=jnp.float32), approximate=True
     ).astype(jnp.bfloat16)

time: 823 us -> 870 us (1.057)
  waiting for transfers between devices: 735 us -> 767 us
  starting transfers between devices: 0.12 us -> 11.8 us
    all_to_all x0 -> x1, waiting for transfers between devices: none -> 82.5 us  [shards(): lax.all_to_all(jnp.stack([normed] * lax.axis_size(('req', 'hid'))), ('req...]
    all_gather x1 -> x0, waiting for transfers between devices: 55.2 us -> none  [shards(): gathered = lax.all_gather(normed, ('req', 'hid'), axis=0, tiled=True)]
    all_to_all x0 -> x1, starting transfers between devices: none -> 11.7 us  [shards(): lax.all_to_all(jnp.stack([normed] * lax.axis_size(('req', 'hid'))), ('req...]
where the time goes in v1:
time: 870 us; the launch traced here: 869 us
  waiting for transfers between devices  767 us (88%)
  matrix products  38.6 us (4%)
  local copies, waits for them, and re-layouts  30.6 us (4%)
  between operations  14.4 us (2%)
  starting transfers between devices  11.8 us (1%)
    reduce_scatter x1, waiting for transfers between devices, shards(): lax.psum_scatter(jnp.dot(hidden_units, down_weight, preferred_element_typ...  667 us
    all_to_all x1, waiting for transfers between devices, shards(): lax.all_to_all(jnp.stack([normed] * lax.axis_size(('req', 'hid'))), ('req...  82.5 us
    unnamed x13, local copies, waits for them, and re-layouts  17.6 us
  transfers between devices with their start and end apart: 3, of which 3 were waited for; matrix products, arithmetic and copies ran while one was open for 4% of the time, Pallas kernels for 0%

profile of v1, /device:TPU:0, one launch (start us, length us, event | category | flops | bytes accessed | tf_op | source)
XLA Modules:
  0.0 869.5 jit_solution(1073615240594041712)
XLA Ops:
  7.2 0.9 reshape.244
  8.1 1.0 convert_reduce_fusion
  9.1 1.1 multiply_reduce_fusion.2
  10.2 0.1 div.23
  10.3 0.1 rsqrt.20
  10.4 0.8 multiply_convert_fusion
  11.2 4.3 stack.7
  15.4 11.7 %all-to-all-start = ((bf16[128,8,4096]{2,1,0:T(8,128)(2,1)}), bf16[128,8,4096]{2,1,0:T(8,128)(2,1)}, u32[]{:S(2)}, u32[]{:S(2)}) async-start(bf16[128,8,4096]{2,1,0:T(8,128)(2,1)} %stack.7), calls=%async_computation | async-start | bytes 16777216 | tf_op jit(solution)/shard_map/all_to_all | solution.py:57
  27.2 16.9 %copy.120 = bf16[4096,3,512]{0,2,1:T(8,128)(2,1)} copy(bf16[4096,3,512]{2,0,1:T(8,128)(2,1)} %param.16) | data formatting | bytes 25165824 | tf_op args[2]
  44.2 0.1 broadcast_add_fusion
  44.3 0.1 iota_compare_fusion
  44.3 0.3 multiply_cosine_fusion
  44.6 0.1 iota_compare_fusion.1
  44.7 82.5 %all-to-all-done = bf16[128,8,4096]{2,1,0:T(8,128)(2,1)} async-done(((bf16[128,8,4096]{2,1,0:T(8,128)(2,1)}), bf16[128,8,4096]{2,1,0:T(8,128)(2,1)}, u32[]{:S(2)}, u32[]{:S(2)}) %all-to-all-start) | async-done | bytes 8388640 | tf_op jit(solution)/shard_map/all_to_all | solution.py:57
  127.3 8.7 convolution_convert_fusion.1
  135.9 0.1 reshape.247
  136.0 0.2 copy.209
  136.2 0.1 reshape.248
  136.3 0.1 slice.72
  136.4 0.1 slice.55
  136.5 0.1 copy.122
  136.7 0.3 multiply_subtract_fusion
  137.0 0.4 maximum_convert_fusion
  137.4 2.0 copy.123
  139.4 0.1 copy.128
  139.5 0.1 copy.133
  139.6 0.3 subtract_convert_fusion
  140.0 0.4 pad_maximum_fusion
  140.3 0.1 copy.134
  140.4 0.1 copy.124
  140.5 0.1 pad_maximum_fusion.1
  140.6 0.2 fusion.65
  140.8 0.1 copy.137
  140.9 2.4 select_reduce_fusion
  143.3 0.1 copy.132
  143.4 1.9 concatenate.16
  145.4 3.6 fusion.91
  149.0 0.1 reshape.253
  149.1 0.1 copy.140
  149.2 0.1 fusion.70
  149.3 0.1 copy.143
  149.4 0.1 fusion.89
  149.5 0.3 fusion.73
  149.8 0.1 copy.148
  149.9 0.3 fusion.39
  150.2 0.1 reshape.260
  150.3 0.1 copy.147
  150.4 0.1 copy.141
  150.5 3.0 fusion.21
  153.6 0.1 reshape.252
  153.7 0.1 copy.151
  153.8 0.1 copy.146
  153.9 2.0 fusion.29
  156.0 0.2 fusion.32
  156.3 4.0 convolution_convert_fusion
  160.4 14.4 %fusion.54 = f32[1024,4096]{1,0:T(8,128)} fusion(bf16[128,4096]{1,0:T(8,128)(2,1)S(1)} %copy-done, bf16[4096,128]{1,0:T(8,128)(2,1)S(1)} %copy-done.1, bf16[128,8,4096]{2,1,0:T(8,128)(2,1)} %all-to-all-done), kind=kOutput, calls=%fused_computation.42 | convolution fusion | flops 2148663296 | bytes 27262976 | tf_op jit(solution)/shard_map/dot_general | solution.py:155
  174.9 0.7 copy-done.3
  175.6 17.0 %reduce-scatter.5.cloned.1.call-done = bf16[8,4096]{1,0:T(8,128)(2,1)} async-done(((bf16[64,4096]{1,0:T(8,128)(2,1)}), bf16[8,4096]{1,0:T(8,128)(2,1)}) %reduce-scatter.5.cloned.1.call-update) | async-done | bytes 65552 | tf_op jit(solution)/shard_map/reduce_scatter | solution.py:160
  192.5 667.3 %reduce-scatter.3.cloned.1.call-done = f32[8,4096]{1,0:T(8,128)} async-done(((f32[1024,4096]{1,0:T(8,128)}), f32[8,4096]{1,0:T(8,128)}) %reduce-scatter.3.cloned.1.call-update) | async-done | bytes 131088 | tf_op jit(solution)/shard_map/reduce_scatter | solution.py:154
  859.8 1.1 fusion.90
  860.8 0.2 multiply_reduce_fusion.1
  861.1 0.2 multiply_reduce_fusion
  861.3 0.7 reshape.263
  862.0 0.7 reshape.264
  (31 shorter events, 0.4 us)
Async XLA Ops:
  7.2 153.2 %copy-start = (bf16[128,4096]{1,0:T(8,128)(2,1)S(1)}, bf16[128,4096]{1,0:T(8,128)(2,1)}, u32[]{:S(2)}) copy-start(bf16[128,4096]{1,0:T(8,128)(2,1)} %param.19) | copy-start | bytes 3145732
  15.4 111.8 %all-to-all-start = ((bf16[128,8,4096]{2,1,0:T(8,128)(2,1)}), bf16[128,8,4096]{2,1,0:T(8,128)(2,1)}, u32[]{:S(2)}, u32[]{:S(2)}) async-start(bf16[128,8,4096]{2,1,0:T(8,128)(2,1)} %stack.7), calls=%async_computation | async-start | bytes 16777216 | tf_op jit(solution)/shard_map/all_to_all | solution.py:57
  27.1 165.4 %reduce-scatter.5.cloned.1.call-start = ((), (), s32[]{:S(2)}) async-start(), calls=%async_computation.4 | async-start | bytes 589824 | tf_op jit(solution)/shard_map/reduce_scatter | solution.py:160
  27.2 17.0 %copy-start.4 = (s32[2,16]{1,0:T(2,128)S(1)}, s32[2,16]{1,0:T(2,128)}, u32[]{:S(2)}) copy-start(s32[2,16]{1,0:T(2,128)} %param.27) | copy-start | bytes 388
  27.2 17.0 %copy-start.5 = (s32[2]{0:T(128)S(1)}, s32[2]{0:T(128)}, u32[]{:S(2)}) copy-start(s32[2]{0:T(128)} %param.26) | copy-start | bytes 28
  155.9 4.5 copy-start.1
  160.3 699.4 %reduce-scatter.3.cloned.1.call-start = ((), (), s32[]{:S(2)}) async-start(), calls=%async_computation.3 | async-start | bytes 16908288 | tf_op jit(solution)/shard_map/reduce_scatter | solution.py:154
  174.9 0.7 copy-start.3
  174.9 686.2 %copy-start.2 = (f32[4096]{0:T(1024)S(1)}, f32[4096]{0:T(1024)}, u32[]{:S(2)}) copy-start(f32[4096]{0:T(1024)} %param.20) | copy-start | bytes 49156
Sparse Core Ops, SparseCore 0:
  160.5 32.0 reduce-scatter.4
  195.0 664.7 reduce-scatter.2
